TPU v7x, 32 devices: a whole 2x2x4 slice. The times are simulated.
32 devices in a mesh: row: 4 (over z), col: 8 (over y, x, core).
Axes of the slice: x: 2, y: 2, z: 4, core: 2. Of those that a mesh axis runs over, the one named last changes fastest.
Arguments:
- features: bfloat16 [8192, 512], P(('row', 'col')), may hold values from -6 to 6
- tile_values: bfloat16 [32, 16, 128, 128], P(('row', 'col')), may hold values from -0.21875 to 0.21875
- tile_blocks: int32 [32, 16, 2], P(('row', 'col')), may hold values from 0 to 63, as said below
- tile_count: int32 [32], P(('row', 'col')), may hold values from 1 to 16, as said below
- needed: int32 [32, 4], P(('row', 'col')), may hold values from 0 to 1
- weight_one: bfloat16 [512, 512], replicated, may hold values from -0.25 to 0.25
- weight_two: bfloat16 [512, 512], replicated, may hold values from -0.25 to 0.25
Outputs:
- nodes_out: bfloat16 [8192, 512], P(('row', 'col'))
Inputs may be any that keep to these rules, and one draw needn't show every extreme that they name: `tile_blocks`: every row block of device d lies among the row blocks owned by the devices that share its index along row; for each device e along col in device d's row, all live or dead tiles of device d whose row block is owned by e name the same one of e's 2 blocks; the last device's first slot names the last block. `tile_count`: some device in every draw has all 16 slots live.
All inputs are finite; a program needn't handle non-finite values.
Results may differ from a plain program's by a relative error of at most 0.017.
Values may be sent and summed in bfloat16 or wider, within the bound.
No kernel may reach another device: no remote copies, remote signals or barrier semaphores. Data moves between devices by JAX's collectives and lax.ppermute only.
A program may use at most 64 MiB of HBM per device.

v0:
```python
import jax
import jax.numpy as jnp
from jax import lax
from jax.sharding import PartitionSpec as P


def body(features, tile_values, tile_blocks, tile_count, needed, weight_one, weight_two):
    col_count = lax.axis_size("col")
    adjacency = tile_values[0]
    blocks_here = tile_blocks[0]
    tile_slots = adjacency.shape[0]
    tile_size = adjacency.shape[1]
    feat_width = features.shape[1]
    per_device = features.shape[0] // tile_size
    alive_mask = jnp.arange(tile_slots) < tile_count[0]
    source_owner = blocks_here[:, 1]
    wanted = needed[0]
    target = blocks_here[:, 0] // per_device % col_count
    local_block = blocks_here[:, 0] % per_device
    dest_hit = (target[:, None] == jnp.arange(col_count)[None, :]) & alive_mask[:, None]
    dest_weights = dest_hit.astype(jnp.bfloat16)
    both_weights = jnp.concatenate([dest_weights, dest_weights], axis=0)
    send_block = jnp.max(jnp.where(dest_hit, local_block[:, None], 0), axis=0)
    hidden = features
    for layer_index, weight in enumerate((weight_one, weight_two)):
        owned = hidden.reshape(per_device, tile_size, feat_width)
        panel_rows = lax.all_gather(owned, "row", axis=0, tiled=True)
        operands = panel_rows[source_owner * per_device + wanted[source_owner]]
        products = jnp.einsum(
            "tmk,tkf->tmf", adjacency, operands, preferred_element_type=jnp.float32
        )
        upper_part = products.astype(jnp.bfloat16)
        lower_part = (products - upper_part.astype(jnp.float32)).astype(jnp.bfloat16)
        stacked = jnp.concatenate([upper_part, lower_part], axis=0)
        partial_value = jnp.einsum(
            "tc,tmf->cmf", both_weights, stacked, preferred_element_type=jnp.float32
        )
        partial_value = partial_value.astype(jnp.bfloat16)
        arrived_parts = lax.all_to_all(
            partial_value, "col", split_axis=0, concat_axis=0, tiled=True
        )
        picked = lax.all_to_all(send_block, "col", split_axis=0, concat_axis=0, tiled=True)
        chooser = (picked[:, None] == jnp.arange(per_device)[None, :]).astype(jnp.bfloat16)
        summed = jnp.einsum(
            "sb,smf->bmf", chooser, arrived_parts, preferred_element_type=jnp.float32
        )
        mixed = summed.astype(jnp.bfloat16).reshape(per_device * tile_size, feat_width)
        result = jnp.dot(mixed, weight, preferred_element_type=jnp.float32)
        if layer_index == 0:
            hidden = jnp.maximum(result, 0.0).astype(jnp.bfloat16)
        else:
            hidden = result.astype(jnp.bfloat16)
    return hidden


def solution(mesh):
    placed = (
        P(("row", "col"), None),
        P(("row", "col"), None, None, None),
        P(("row", "col"), None, None),
        P(("row", "col")),
        P(("row", "col"), None),
        P(),
        P(),
    )
    return jax.shard_map(
        body, mesh=mesh, in_specs=placed, out_specs=P(("row", "col"), None), check_vma=False
    )
```

profile of v0, /device:TPU:0, one launch (start us, length us, event | category | flops | bytes accessed | tf_op | source)
XLA Modules:
  0.0 147.8 jit_solution(7393868171918821235)
XLA Ops:
  6.5 0.0 copy-start
  6.5 0.0 all-gather.3.cloned.1.call-start
  6.5 0.7 all-gather.3.cloned.1.call-update
  7.9 0.7 fusion.13
  8.6 0.8 fusion.12
  9.4 0.1 select_reduce_fusion
  9.5 0.7 copy.23
  10.2 5.2 %all-to-all-start = ((s32[8,1,1]{2,1,0:T(1,128)}), s32[8,1,1]{2,1,0:T(1,128)S(1)}, u32[]{:S(2)}, u32[]{:S(2)}) async-start(s32[8,1,1]{2,1,0:T(1,128)} %copy.23), calls=%async_computation | async-start | bytes 8192 | tf_op jit(solution)/shard_map/all_to_all | solution.py:42
  15.4 1.3 gather_fusion
  16.7 0.7 fusion.16
  17.4 22.2 %all-gather.3.cloned.1.call-done = bf16[8,128,512]{2,1,0:T(8,128)(2,1)} async-done(((bf16[2,128,512]{2,1,0:T(8,128)(2,1)}), bf16[8,128,512]{2,1,0:T(8,128)(2,1)}) %all-gather.3.cloned.1.call-update) | async-done | bytes 1048592 | tf_op jit(solution)/shard_map/all_gather | solution.py:27
  39.6 1.9 %gather_fusion.1 = bf16[16,128,512]{2,1,0:T(8,128)(2,1)S(1)} fusion(bf16[8,128,512]{2,1,0:T(8,128)(2,1)} %all-gather.3.cloned.1.call-done, s32[1024]{0:T(1024)S(1)} %pad_clamp_fusion), kind=kCustom, calls=%fused_computation.1 | custom fusion | bytes 4194368 | tf_op jit(solution)/shard_map/gather | solution.py:28
  41.5 0.0 copy-done
  41.5 1.0 fusion.1
  42.5 2.3 %pad_maximum_fusion = bf16[32,128,512]{1,2,0:T(8,128)(2,1)} fusion(bf16[16,128,512]{1,2,0:T(8,128)(2,1)S(1)} %get-tuple-element.9, bf16[16,128,512]{1,2,0:T(8,128)(2,1)S(1)} %get-tuple-element.10), kind=kLoop, calls=%fused_computation.3 | loop fusion | flops 2097152 | bytes 8388608 | tf_op jit(solution)/shard_map/concatenate | solution.py:34
  44.8 8.0 %copy.25 = bf16[32,128,512]{2,0,1:T(8,128)(2,1)} copy(bf16[32,128,512]{1,2,0:T(8,128)(2,1)} %pad_maximum_fusion) | data formatting | bytes 8388608 | tf_op jit(solution)/shard_map/concatenate | solution.py:34
  52.8 2.9 %convolution_convert_fusion.1 = bf16[8,128,512]{2,0,1:T(8,128)(2,1)S(1)} fusion(bf16[32,128,512]{2,0,1:T(8,128)(2,1)} %copy.25, pred[16,8]{0,1:T(8,128)(4,1)S(1)} %fusion.9), kind=kOutput, calls=%fused_computation.12 | convolution fusion | flops 34078976 | bytes 5243008 | tf_op jit(solution)/shard_map/tc,tmf->cmf/dot_general | solution.py:35
  55.7 1.3 copy.26
  57.0 0.0 copy-start.1
  57.0 0.0 all-to-all-done
  57.0 3.8 %all-to-all-start.1 = ((bf16[8,128,512]{2,1,0:T(8,128)(2,1)}), bf16[8,128,512]{2,1,0:T(8,128)(2,1)S(1)}, u32[]{:S(2)}, u32[]{:S(2)}) async-start(bf16[8,128,512]{2,1,0:T(8,128)(2,1)} %copy.26), calls=%async_computation.1 | async-start | bytes 2097152 | tf_op jit(solution)/shard_map/all_to_all | solution.py:39
  60.8 0.0 all-gather.5.cloned.1.call-start
  60.8 0.2 reduce
  61.0 15.1 %all-to-all-done.1 = bf16[8,128,512]{2,1,0:T(8,128)(2,1)S(1)} async-done(((bf16[8,128,512]{2,1,0:T(8,128)(2,1)}), bf16[8,128,512]{2,1,0:T(8,128)(2,1)S(1)}, u32[]{:S(2)}, u32[]{:S(2)}) %all-to-all-start.1) | async-done | bytes 1048608 | tf_op jit(solution)/shard_map/all_to_all | solution.py:39
  76.2 0.7 convolution_convert_fusion.4
  77.0 0.0 copy-done.1
  77.0 1.0 fusion.2
  78.0 0.0 all-gather.5.cloned.1.call-update
  78.0 25.8 %all-gather.5.cloned.1.call-done = bf16[8,128,512]{2,1,0:T(8,128)(2,1)} async-done(((bf16[2,128,512]{2,1,0:T(8,128)(2,1)}), bf16[8,128,512]{2,1,0:T(8,128)(2,1)}) %all-gather.5.cloned.1.call-update) | async-done | bytes 1048592 | tf_op jit(solution)/shard_map/all_gather | solution.py:27
  103.8 1.9 %gather_fusion.2 = bf16[16,128,512]{2,1,0:T(8,128)(2,1)S(1)} fusion(bf16[8,128,512]{2,1,0:T(8,128)(2,1)} %all-gather.5.cloned.1.call-done, s32[1024]{0:T(1024)S(1)} %pad_clamp_fusion), kind=kCustom, calls=%fused_computation.2 | custom fusion | bytes 4194368 | tf_op jit(solution)/shard_map/gather | solution.py:28
  105.7 1.0 fusion
  106.7 2.3 %pad_maximum_fusion.1 = bf16[32,128,512]{1,2,0:T(8,128)(2,1)} fusion(bf16[16,128,512]{1,2,0:T(8,128)(2,1)S(1)} %get-tuple-element.5, bf16[16,128,512]{1,2,0:T(8,128)(2,1)S(1)} %get-tuple-element.6), kind=kLoop, calls=%fused_computation.4 | loop fusion | flops 2097152 | bytes 8388608 | tf_op jit(solution)/shard_map/concatenate | solution.py:34
  109.0 8.0 %copy.30 = bf16[32,128,512]{2,0,1:T(8,128)(2,1)} copy(bf16[32,128,512]{1,2,0:T(8,128)(2,1)} %pad_maximum_fusion.1) | data formatting | bytes 8388608 | tf_op jit(solution)/shard_map/concatenate | solution.py:34
  117.0 2.9 %convolution_convert_fusion = bf16[8,128,512]{2,0,1:T(8,128)(2,1)S(1)} fusion(bf16[32,128,512]{2,0,1:T(8,128)(2,1)} %copy.30, pred[16,8]{0,1:T(8,128)(4,1)S(1)} %fusion.9), kind=kOutput, calls=%fused_computation.11 | convolution fusion | flops 34078976 | bytes 5243008 | tf_op jit(solution)/shard_map/tc,tmf->cmf/dot_general | solution.py:35
  119.9 0.3 copy.31
  120.2 0.0 copy-start.2
  120.2 18.9 %all_to_all.20 = bf16[8,128,512]{2,1,0:T(8,128)(2,1)S(1)} all-to-all(bf16[8,128,512]{2,1,0:T(8,128)(2,1)S(1)} %copy.31), channel_id=1, replica_groups=mesh['row'=4,'col'=8] {'col'}, dimensions={0} | all-to-all | bytes 2097152 | tf_op jit(solution)/shard_map/all_to_all | solution.py:39
  139.2 0.7 convolution_convert_fusion.3
  139.9 0.0 copy-done.2
  140.0 1.0 convolution_convert_fusion.2
  (6 shorter events, 0.1 us)
Async XLA Ops:
  6.5 35.0 %copy-start = (bf16[1,16,128,128]{3,2,1,0:T(8,128)(2,1)S(1)}, bf16[1,16,128,128]{3,2,1,0:T(8,128)(2,1)}, u32[]{:S(2)}) copy-start(bf16[1,16,128,128]{3,2,1,0:T(8,128)(2,1)} %param.8) | copy-start | bytes 1572868
  6.5 33.1 %all-gather.3.cloned.1.call-start = ((), (), s32[]{:S(2)}) async-start(), calls=%async_computation.3 | async-start | bytes 1310720 | tf_op jit(solution)/shard_map/all_gather | solution.py:27
  10.2 46.8 %all-to-all-start = ((s32[8,1,1]{2,1,0:T(1,128)}), s32[8,1,1]{2,1,0:T(1,128)S(1)}, u32[]{:S(2)}, u32[]{:S(2)}) async-start(s32[8,1,1]{2,1,0:T(1,128)} %copy.23), calls=%async_computation | async-start | bytes 8192 | tf_op jit(solution)/shard_map/all_to_all | solution.py:42
  57.0 20.0 %copy-start.1 = (bf16[512,512]{1,0:T(8,128)(2,1)S(1)}, bf16[512,512]{1,0:T(8,128)(2,1)}, u32[]{:S(2)}) copy-start(bf16[512,512]{1,0:T(8,128)(2,1)} %param.12) | copy-start | bytes 1572868
  57.0 19.2 %all-to-all-start.1 = ((bf16[8,128,512]{2,1,0:T(8,128)(2,1)}), bf16[8,128,512]{2,1,0:T(8,128)(2,1)S(1)}, u32[]{:S(2)}, u32[]{:S(2)}) async-start(bf16[8,128,512]{2,1,0:T(8,128)(2,1)} %copy.26), calls=%async_computation.1 | async-start | bytes 2097152 | tf_op jit(solution)/shard_map/all_to_all | solution.py:39
  60.8 43.0 %all-gather.5.cloned.1.call-start = ((), (), s32[]{:S(2)}) async-start(), calls=%async_computation.4 | async-start | bytes 1310720 | tf_op jit(solution)/shard_map/all_gather | solution.py:27
  120.2 19.7 %copy-start.2 = (bf16[512,512]{1,0:T(8,128)(2,1)S(1)}, bf16[512,512]{1,0:T(8,128)(2,1)}, u32[]{:S(2)}) copy-start(bf16[512,512]{1,0:T(8,128)(2,1)} %param.13) | copy-start | bytes 1572868
Sparse Core Ops, SparseCore 0:
  8.9 30.6 all-gather.2
  78.1 25.6 all-gather.4
where the time goes:
time: 149 us; the launch traced here: 148 us
  waiting for transfers between devices  63.9 us (43%)
  local copies, waits for them, and re-layouts  23.4 us (16%)
  blocking collectives  18.9 us (13%)
  between operations  14.2 us (10%)
  matrix products  11.3 us (8%)
  starting transfers between devices  9 us (6%)
  other arithmetic  7.17 us (5%)
    all_gather x2, waiting for transfers between devices, body(): panel_rows = lax.all_gather(owned, 'row', axis=0, tiled=True)  48 us
    all_to_all x1, blocking collectives, body(): lax.all_to_all(partial_value, 'col', split_axis=0, concat_axis=0, tiled=T...  18.9 us
    concatenate x2, local copies, waits for them, and re-layouts, body(): stacked = jnp.concatenate([upper_part, lower_part], axis=0)  15.9 us
    all_to_all x1, waiting for transfers between devices, body(): lax.all_to_all(partial_value, 'col', split_axis=0, concat_axis=0, tiled=T...  15.1 us
    dot_general x2, matrix products, body(): jnp.einsum('tc,tmf->cmf', both_weights, stacked, preferred_element_type=j...  5.81 us
    all_to_all x1, starting transfers between devices, body(): lax.all_to_all(send_block, 'col', split_axis=0, concat_axis=0, tiled=True)  5.17 us
    gather x3, local copies, waits for them, and re-layouts, body(): operands = panel_rows[source_owner * per_device + wanted[source_owner]]  5.12 us
    concatenate x2, other arithmetic, body(): stacked = jnp.concatenate([upper_part, lower_part], axis=0)  4.64 us
  transfers between devices with their start and end apart: 4, of which 3 were waited for; matrix products, arithmetic and copies ran while one was open for 15% of the time, Pallas kernels for 0%

commit v1 on v0

--- a/solution.py
+++ b/solution.py
@@ -2,6 +2,22 @@
 import jax.numpy as jnp
 from jax import lax
 from jax.sharding import PartitionSpec as P
+
+
+def exchange_in_pairs(x, axis, split, join):
+    ways, here = (lax.axis_size(axis), lax.axis_index(axis))
+    width = x.shape[split] // ways
+    dims = list(x.shape)
+    dims[split] = width
+    height = dims[join]
+    dims[join] = height * ways
+    full = jnp.zeros(dims, x.dtype)
+    for mask in range(ways):
+        part = lax.dynamic_slice_in_dim(x, (here ^ mask) * width, width, axis=split)
+        if mask:
+            part = lax.ppermute(part, axis, [(d, d ^ mask) for d in range(ways)])
+        full = lax.dynamic_update_slice_in_dim(full, part, (here ^ mask) * height, axis=join)
+    return full
 
 
 def body(features, tile_values, tile_blocks, tile_count, needed, weight_one, weight_two):
@@ -39,7 +55,7 @@
         arrived_parts = lax.all_to_all(
             partial_value, "col", split_axis=0, concat_axis=0, tiled=True
         )
-        picked = lax.all_to_all(send_block, "col", split_axis=0, concat_axis=0, tiled=True)
+        picked = exchange_in_pairs(send_block, "col", 0, 0)
         chooser = (picked[:, None] == jnp.arange(per_device)[None, :]).astype(jnp.bfloat16)
         summed = jnp.einsum(
             "sb,smf->bmf", chooser, arrived_parts, preferred_element_type=jnp.float32

time: 149 us -> 154 us (1.034)
  local copies, waits for them, and re-layouts: 23.4 us -> 28.5 us
  starting transfers between devices: 9 us -> 11 us
    all_to_all x1, waiting for transfers between devices: 15.1 us -> 0.01 us  [body(): lax.all_to_all(partial_value, 'col', split_axis=0, concat_axis=0, tiled=T...]
    all_gather x2, waiting for transfers between devices: 48 us -> 55.4 us  [body(): panel_rows = lax.all_gather(owned, 'row', axis=0, tiled=True)]
    ppermute x0 -> x7, starting transfers between devices: none -> 7.13 us  [exchange_in_pairs(): part = lax.ppermute(part, axis, [(d, d ^ mask) for d in range(ways)])]
    ppermute x0 -> x7, waiting for transfers between devices: none -> 6.49 us  [exchange_in_pairs(): part = lax.ppermute(part, axis, [(d, d ^ mask) for d in range(ways)])]
    all_to_all x1 -> x0, starting transfers between devices: 5.17 us -> none  [body(): lax.all_to_all(send_block, 'col', split_axis=0, concat_axis=0, tiled=True)]
    dynamic_update_slice x0 -> x7, local copies, waits for them, and re-layouts: none -> 5.02 us  [exchange_in_pairs(): lax.dynamic_update_slice_in_dim(full, part, (here ^ mask) * height, axis=...]
  transfers between devices with their start and end apart: 4 -> 10, of which waited for: 3 -> 3; matrix products, arithmetic and copies ran while one was open for 15% -> 6% of each run, Pallas kernels for 0% -> 0%
where the time goes in v1:
time: 154 us; the launch traced here: 153 us
  waiting for transfers between devices  62.7 us (41%)
  local copies, waits for them, and re-layouts  28.5 us (19%)
  blocking collectives  18.9 us (12%)
  between operations  14.2 us (9%)
  matrix products  11.3 us (7%)
  starting transfers between devices  11 us (7%)
  other arithmetic  6.92 us (4%)
    all_gather x2, waiting for transfers between devices, body(): panel_rows = lax.all_gather(owned, 'row', axis=0, tiled=True)  55.4 us
    all_to_all x1, blocking collectives, body(): lax.all_to_all(partial_value, 'col', split_axis=0, concat_axis=0, tiled=T...  18.9 us
    concatenate x2, local copies, waits for them, and re-layouts, body(): stacked = jnp.concatenate([upper_part, lower_part], axis=0)  15.9 us
    ppermute x7, starting transfers between devices, exchange_in_pairs(): part = lax.ppermute(part, axis, [(d, d ^ mask) for d in range(ways)])  7.13 us
    ppermute x7, waiting for transfers between devices, exchange_in_pairs(): part = lax.ppermute(part, axis, [(d, d ^ mask) for d in range(ways)])  6.49 us
    dot_general x2, matrix products, body(): jnp.einsum('tc,tmf->cmf', both_weights, stacked, preferred_element_type=j...  5.81 us
    gather x3, local copies, waits for them, and re-layouts, body(): operands = panel_rows[source_owner * per_device + wanted[source_owner]]  5.12 us
    dynamic_update_slice x7, local copies, waits for them, and re-layouts, exchange_in_pairs(): lax.dynamic_update_slice_in_dim(full, part, (here ^ mask) * height, axis=...  5.02 us
  transfers between devices with their start and end apart: 10, of which 3 were waited for; matrix products, arithmetic and copies ran while one was open for 6% of the time, Pallas kernels for 0%

profile of v1, /device:TPU:0, one launch (start us, length us, event | category | flops | bytes accessed | tf_op | source)
XLA Modules:
  0.0 153.4 jit_solution(2227590795820715001)
XLA Ops:
  6.5 0.7 all-gather.3.cloned.1.call-update
  7.9 0.7 fusion.13
  8.6 0.8 fusion.12
  9.4 1.3 gather_fusion
  10.7 0.7 fusion.16
  11.4 28.2 %all-gather.3.cloned.1.call-done = bf16[8,128,512]{2,1,0:T(8,128)(2,1)} async-done(((bf16[2,128,512]{2,1,0:T(8,128)(2,1)}), bf16[8,128,512]{2,1,0:T(8,128)(2,1)}) %all-gather.3.cloned.1.call-update) | async-done | bytes 1048592 | tf_op jit(solution)/shard_map/all_gather | solution.py:43
  39.6 1.9 %gather_fusion.1 = bf16[16,128,512]{2,1,0:T(8,128)(2,1)S(1)} fusion(bf16[8,128,512]{2,1,0:T(8,128)(2,1)} %all-gather.3.cloned.1.call-done, s32[1024]{0:T(1024)S(1)} %pad_clamp_fusion), kind=kCustom, calls=%fused_computation.1 | custom fusion | bytes 4194368 | tf_op jit(solution)/shard_map/gather | solution.py:44
  41.5 1.0 fusion.1
  42.5 2.3 %pad_maximum_fusion = bf16[32,128,512]{1,2,0:T(8,128)(2,1)} fusion(bf16[16,128,512]{1,2,0:T(8,128)(2,1)S(1)} %get-tuple-element.9, bf16[16,128,512]{1,2,0:T(8,128)(2,1)S(1)} %get-tuple-element.10), kind=kLoop, calls=%fused_computation.3 | loop fusion | flops 2097152 | bytes 8388608 | tf_op jit(solution)/shard_map/concatenate | solution.py:50
  44.8 7.9 %copy.13 = bf16[32,128,512]{2,0,1:T(8,128)(2,1)} copy(bf16[32,128,512]{1,2,0:T(8,128)(2,1)} %pad_maximum_fusion) | data formatting | bytes 8388608 | tf_op jit(solution)/shard_map/concatenate | solution.py:50
  52.7 2.9 %convolution_convert_fusion.1 = bf16[8,128,512]{2,0,1:T(8,128)(2,1)S(1)} fusion(bf16[32,128,512]{2,0,1:T(8,128)(2,1)} %copy.13, pred[16,8]{0,1:T(8,128)(4,1)S(1)} %fusion.9), kind=kOutput, calls=%fused_computation.12 | convolution fusion | flops 34078976 | bytes 5243008 | tf_op jit(solution)/shard_map/tc,tmf->cmf/dot_general | solution.py:51
  55.7 1.3 copy.14
  57.0 3.8 %all-to-all-start = ((bf16[8,128,512]{2,1,0:T(8,128)(2,1)}), bf16[8,128,512]{2,1,0:T(8,128)(2,1)S(1)}, u32[]{:S(2)}, u32[]{:S(2)}) async-start(bf16[8,128,512]{2,1,0:T(8,128)(2,1)} %copy.14), calls=%async_computation | async-start | bytes 2097152 | tf_op jit(solution)/shard_map/all_to_all | solution.py:55
  60.8 0.0 all-gather.5.cloned.1.call-start
  60.8 0.1 select_reduce_fusion
  61.0 0.7 fusion.21
  61.7 0.4 collective-permute-start
  62.1 1.7 %collective-permute-start.1 = (s32[1]{0:T(128)}, s32[1]{0:T(128)}, u32[]{:S(2)}, u32[]{:S(2)}) collective-permute-start(s32[1]{0:T(128)} %get-tuple-element.18), channel_id=1, source_target_pairs={{0,2},{1,3},{2,0},{3,1},{4,6},{5,7},{6,4},{7,5},{8,10},{9,11},{10,... | collective-permute-start | bytes 20 | tf_op jit(solution)/shard_map/ppermute | solution.py:18
  63.8 0.0 collective-permute-start.2
  63.8 1.7 %collective-permute-start.3 = (s32[1]{0:T(128)}, s32[1]{0:T(128)}, u32[]{:S(2)}, u32[]{:S(2)}) collective-permute-start(s32[1]{0:T(128)} %get-tuple-element.16), channel_id=1, source_target_pairs={{0,4},{1,5},{2,6},{3,7},{4,0},{5,1},{6,2},{7,3},{8,12},{9,13},{10,... | collective-permute-start | bytes 20 | tf_op jit(solution)/shard_map/ppermute | solution.py:18
  65.5 0.1 collective-permute-start.4
  65.6 0.0 collective-permute-done
  65.6 2.6 %collective-permute-start.5 = (s32[1]{0:T(128)}, s32[1]{0:T(128)}, u32[]{:S(2)}, u32[]{:S(2)}) collective-permute-start(s32[1]{0:T(128)} %get-tuple-element.14), channel_id=1, source_target_pairs={{0,6},{1,7},{2,4},{3,5},{4,2},{5,3},{6,0},{7,1},{8,14},{9,15},{10,... | collective-permute-start | bytes 20 | tf_op jit(solution)/shard_map/ppermute | solution.py:18
  68.2 0.7 dynamic_update_slice.49
  68.9 6.5 %collective-permute-done.1 = s32[1]{0:T(128)} collective-permute-done((s32[1]{0:T(128)}, s32[1]{0:T(128)}, u32[]{:S(2)}, u32[]{:S(2)}) %collective-permute-start.1) | collective-permute-done | bytes 36 | tf_op jit(solution)/shard_map/ppermute | solution.py:18
  75.4 0.6 collective-permute-start.6
  76.0 0.7 dynamic_update_slice.50
  76.7 0.0 collective-permute-done.2
  76.7 0.7 dynamic_update_slice.51
  77.4 0.7 dynamic_update_slice.52
  78.2 0.0 collective-permute-done.4
  78.2 0.7 dynamic_update_slice.53
  78.9 0.7 dynamic_update_slice.54
  79.6 0.7 dynamic_update_slice.55
  80.4 0.7 convolution_convert_fusion.4
  81.2 1.0 fusion.2
  82.2 0.0 all-gather.5.cloned.1.call-update
  82.2 27.3 %all-gather.5.cloned.1.call-done = bf16[8,128,512]{2,1,0:T(8,128)(2,1)} async-done(((bf16[2,128,512]{2,1,0:T(8,128)(2,1)}), bf16[8,128,512]{2,1,0:T(8,128)(2,1)}) %all-gather.5.cloned.1.call-update) | async-done | bytes 1048592 | tf_op jit(solution)/shard_map/all_gather | solution.py:43
  109.5 1.9 %gather_fusion.2 = bf16[16,128,512]{2,1,0:T(8,128)(2,1)S(1)} fusion(bf16[8,128,512]{2,1,0:T(8,128)(2,1)} %all-gather.5.cloned.1.call-done, s32[1024]{0:T(1024)S(1)} %pad_clamp_fusion), kind=kCustom, calls=%fused_computation.2 | custom fusion | bytes 4194368 | tf_op jit(solution)/shard_map/gather | solution.py:44
  111.4 1.0 fusion
  112.4 2.3 %pad_maximum_fusion.1 = bf16[32,128,512]{1,2,0:T(8,128)(2,1)} fusion(bf16[16,128,512]{1,2,0:T(8,128)(2,1)S(1)} %get-tuple-element.5, bf16[16,128,512]{1,2,0:T(8,128)(2,1)S(1)} %get-tuple-element.6), kind=kLoop, calls=%fused_computation.4 | loop fusion | flops 2097152 | bytes 8388608 | tf_op jit(solution)/shard_map/concatenate | solution.py:50
  114.7 7.9 %copy.18 = bf16[32,128,512]{2,0,1:T(8,128)(2,1)} copy(bf16[32,128,512]{1,2,0:T(8,128)(2,1)} %pad_maximum_fusion.1) | data formatting | bytes 8388608 | tf_op jit(solution)/shard_map/concatenate | solution.py:50
  122.6 2.9 %convolution_convert_fusion = bf16[8,128,512]{2,0,1:T(8,128)(2,1)S(1)} fusion(bf16[32,128,512]{2,0,1:T(8,128)(2,1)} %copy.18, pred[16,8]{0,1:T(8,128)(4,1)S(1)} %fusion.9), kind=kOutput, calls=%fused_computation.11 | convolution fusion | flops 34078976 | bytes 5243008 | tf_op jit(solution)/shard_map/tc,tmf->cmf/dot_general | solution.py:51
  125.5 0.3 copy.19
  125.8 0.0 copy-start.2
  125.8 18.9 %all_to_all.10 = bf16[8,128,512]{2,1,0:T(8,128)(2,1)S(1)} all-to-all(bf16[8,128,512]{2,1,0:T(8,128)(2,1)S(1)} %copy.19), channel_id=1, replica_groups=mesh['row'=4,'col'=8] {'col'}, dimensions={0} | all-to-all | bytes 2097152 | tf_op jit(solution)/shard_map/all_to_all | solution.py:55
  144.8 0.7 convolution_convert_fusion.3
  145.6 1.0 convolution_convert_fusion.2
  (17 shorter events, 0.1 us)
Async XLA Ops:
  6.5 35.0 %copy-start = (bf16[1,16,128,128]{3,2,1,0:T(8,128)(2,1)S(1)}, bf16[1,16,128,128]{3,2,1,0:T(8,128)(2,1)}, u32[]{:S(2)}) copy-start(bf16[1,16,128,128]{3,2,1,0:T(8,128)(2,1)} %param.8) | copy-start | bytes 1572868
  6.5 33.1 %all-gather.3.cloned.1.call-start = ((), (), s32[]{:S(2)}) async-start(), calls=%async_computation.2 | async-start | bytes 1310720 | tf_op jit(solution)/shard_map/all_gather | solution.py:43
  57.0 24.2 %copy-start.1 = (bf16[512,512]{1,0:T(8,128)(2,1)S(1)}, bf16[512,512]{1,0:T(8,128)(2,1)}, u32[]{:S(2)}) copy-start(bf16[512,512]{1,0:T(8,128)(2,1)} %param.12) | copy-start | bytes 1572868
  57.0 23.4 %all-to-all-start = ((bf16[8,128,512]{2,1,0:T(8,128)(2,1)}), bf16[8,128,512]{2,1,0:T(8,128)(2,1)S(1)}, u32[]{:S(2)}, u32[]{:S(2)}) async-start(bf16[8,128,512]{2,1,0:T(8,128)(2,1)} %copy.14), calls=%async_computation | async-start | bytes 2097152 | tf_op jit(solution)/shard_map/all_to_all | solution.py:55
  60.8 48.7 %all-gather.5.cloned.1.call-start = ((), (), s32[]{:S(2)}) async-start(), calls=%async_computation.3 | async-start | bytes 1310720 | tf_op jit(solution)/shard_map/all_gather | solution.py:43
  61.7 3.9 %collective-permute-start = (s32[1]{0:T(128)}, s32[1]{0:T(128)}, u32[]{:S(2)}, u32[]{:S(2)}) collective-permute-start(s32[1]{0:T(128)} %get-tuple-element.19), channel_id=1, source_target_pairs={{0,1},{1,0},{2,3},{3,2},{4,5},{5,4},{6,7},{7,6},{8,9},{9,8},{10,11... | collective-permute-start | bytes 20 | tf_op jit(solution)/shard_map/ppermute | solution.py:18
  62.1 13.2 %collective-permute-start.1 = (s32[1]{0:T(128)}, s32[1]{0:T(128)}, u32[]{:S(2)}, u32[]{:S(2)}) collective-permute-start(s32[1]{0:T(128)} %get-tuple-element.18), channel_id=1, source_target_pairs={{0,2},{1,3},{2,0},{3,1},{4,6},{5,7},{6,4},{7,5},{8,10},{9,11},{10,... | collective-permute-start | bytes 20 | tf_op jit(solution)/shard_map/ppermute | solution.py:18
  63.8 12.8 %collective-permute-start.2 = (s32[1]{0:T(128)}, s32[1]{0:T(128)}, u32[]{:S(2)}, u32[]{:S(2)}) collective-permute-start(s32[1]{0:T(128)} %get-tuple-element.17), channel_id=1, source_target_pairs={{0,3},{1,2},{2,1},{3,0},{4,7},{5,6},{6,5},{7,4},{8,11},{9,10},{10,... | collective-permute-start | bytes 20 | tf_op jit(solution)/shard_map/ppermute | solution.py:18
  63.8 13.6 %collective-permute-start.3 = (s32[1]{0:T(128)}, s32[1]{0:T(128)}, u32[]{:S(2)}, u32[]{:S(2)}) collective-permute-start(s32[1]{0:T(128)} %get-tuple-element.16), channel_id=1, source_target_pairs={{0,4},{1,5},{2,6},{3,7},{4,0},{5,1},{6,2},{7,3},{8,12},{9,13},{10,... | collective-permute-start | bytes 20 | tf_op jit(solution)/shard_map/ppermute | solution.py:18
  65.5 12.6 %collective-permute-start.4 = (s32[1]{0:T(128)}, s32[1]{0:T(128)}, u32[]{:S(2)}, u32[]{:S(2)}) collective-permute-start(s32[1]{0:T(128)} %get-tuple-element.15), channel_id=1, source_target_pairs={{0,5},{1,4},{2,7},{3,6},{4,1},{5,0},{6,3},{7,2},{8,13},{9,12},{10,... | collective-permute-start | bytes 20 | tf_op jit(solution)/shard_map/ppermute | solution.py:18
  65.6 13.3 %collective-permute-start.5 = (s32[1]{0:T(128)}, s32[1]{0:T(128)}, u32[]{:S(2)}, u32[]{:S(2)}) collective-permute-start(s32[1]{0:T(128)} %get-tuple-element.14), channel_id=1, source_target_pairs={{0,6},{1,7},{2,4},{3,5},{4,2},{5,3},{6,0},{7,1},{8,14},{9,15},{10,... | collective-permute-start | bytes 20 | tf_op jit(solution)/shard_map/ppermute | solution.py:18
  75.4 4.3 %collective-permute-start.6 = (s32[1]{0:T(128)}, s32[1]{0:T(128)}, u32[]{:S(2)}, u32[]{:S(2)}) collective-permute-start(s32[1]{0:T(128)} %get-tuple-element.13), channel_id=1, source_target_pairs={{0,7},{1,6},{2,5},{3,4},{4,3},{5,2},{6,1},{7,0},{8,15},{9,14},{10,... | collective-permute-start | bytes 20 | tf_op jit(solution)/shard_map/ppermute | solution.py:18
  125.8 19.7 %copy-start.2 = (bf16[512,512]{1,0:T(8,128)(2,1)S(1)}, bf16[512,512]{1,0:T(8,128)(2,1)}, u32[]{:S(2)}) copy-start(bf16[512,512]{1,0:T(8,128)(2,1)} %param.13) | copy-start | bytes 1572868
Sparse Core Ops, SparseCore 0:
  8.9 30.6 all-gather.2
  82.3 27.0 all-gather.4
